TPU v7x, 32 devices: a whole 2x2x4 slice. The times are simulated.
32 devices in a mesh: frame: 8 (over y, x, core), chan: 4 (over z).
Axes of the slice: x: 2, y: 2, z: 4, core: 2. Of those that a mesh axis runs over, the one named last changes fastest.
Arguments:
- latent: bfloat16 [8, 512, 2560], P('frame', 'chan'), may hold values from -6 to 6
- spatial_w: bfloat16 [512, 4608], P('chan'), may hold values from -0.09375 to 0.09375
- spatial_b: float32 [512], P('chan'), may hold values from -0.5 to 0.5
- temporal_w: float32 [3, 512], P(None, 'chan'), may hold values from -3 to 3
- temporal_b: float32 [512], P('chan'), may hold values from -1 to 1
Outputs:
- decoded: bfloat16 [8, 512, 2560], P('frame', 'chan')
All inputs are finite; a program needn't handle non-finite values.
Results may differ from a plain program's by a relative error of at most 0.0048.
Values may be sent and summed in bfloat16 or wider, within the bound.
No kernel may reach another device: no remote copies, remote signals or barrier semaphores. Data moves between devices by JAX's collectives and lax.ppermute only.
A program may use at most 64 MiB of HBM per device.

v0:
```python
import jax
import jax.numpy as jnp
from jax import lax
from jax.sharding import PartitionSpec as P

W = 160


def convolve(image, filters, padding):
    return lax.conv_general_dilated(
        image,
        filters,
        (1, 1),
        padding,
        dimension_numbers=("NCHW", "OIHW", "NCHW"),
        preferred_element_type=jnp.float32,
    )


def three_taps(history, values, temporal_w, temporal_b):
    joined = jnp.concatenate([history, values], axis=0).astype(jnp.float32)
    frames = values.shape[0]
    extra = (1,) * (values.ndim - 2)
    taps = temporal_w.reshape((3, 1, temporal_w.shape[1]) + extra)
    bias = temporal_b.reshape((1, temporal_b.shape[0]) + extra)
    total = (
        bias
        + taps[0] * joined[0:frames]
        + taps[1] * joined[1 : frames + 1]
        + taps[2] * joined[2 : frames + 2]
    )
    return total.astype(jnp.bfloat16)


def shards(latent, spatial_w, spatial_b, temporal_w, temporal_b):
    frames, local_chan, pixels = latent.shape
    rows = pixels // W
    full_chan = spatial_w.shape[1] // 9
    shaped_w = spatial_w.reshape(spatial_w.shape[0], 3, 3, full_chan)
    empty = jnp.zeros((frames, spatial_w.shape[0], pixels), jnp.float32)
    piece = lax.all_gather(latent, "chan", axis=1, tiled=True)
    count = piece.shape[1]
    filters = shaped_w.transpose(0, 3, 1, 2)
    image = piece.reshape(frames, count, rows, W)
    summed = empty + convolve(image, filters, ((1, 1), (1, 1))).reshape(
        frames, spatial_w.shape[0], pixels
    )
    spatial = (summed + spatial_b[None, :, None]).astype(jnp.bfloat16)
    band_count = lax.axis_size("frame")
    banded = spatial.reshape(frames, local_chan, band_count, pixels // band_count)
    band = lax.all_to_all(banded, "frame", split_axis=2, concat_axis=0, tiled=True)
    zeros = jnp.zeros((2,) + band.shape[1:], jnp.bfloat16)
    filtered = three_taps(zeros, band, temporal_w, temporal_b)
    result = lax.all_to_all(filtered, "frame", split_axis=0, concat_axis=2, tiled=True)
    decoded = result.reshape(frames, local_chan, pixels)
    return decoded


def solution(mesh):
    placed = (P("frame", "chan", None), P("chan", None), P("chan"), P(None, "chan"), P("chan"))
    return jax.shard_map(
        shards, mesh=mesh, in_specs=placed, out_specs=P("frame", "chan", None), check_vma=False
    )
```

profile of v0, /device:TPU:0, one launch (start us, length us, event | category | flops | bytes accessed | tf_op | source)
XLA Modules:
  0.0 117.0 jit_solution(8465571282082702788)
XLA Ops:
  6.5 0.0 all-gather.2.cloned.1.call-start
  6.5 2.3 %copy.15 = bf16[1,128,2560]{1,2,0:T(8,128)(2,1)} copy(bf16[1,128,2560]{2,1,0:T(8,128)(2,1)} %param.5) | data formatting | bytes 1310720 | tf_op args[0]
  8.8 0.0 all-gather.2.cloned.1.call-update
  8.8 0.7 copy.19
  9.6 57.0 %all-gather.2.cloned.1.call-done = bf16[1,512,2560]{1,2,0:T(8,128)(2,1)} async-done(((bf16[1,128,2560]{1,2,0:T(8,128)(2,1)}), bf16[1,512,2560]{1,2,0:T(8,128)(2,1)}) %all-gather.2.cloned.1.call-update) | async-done | bytes 2621456 | tf_op jit(solution)/shard_map/all_gather | solution.py:41
  66.5 3.2 %copy.25 = bf16[512,16,1,160]{0,1,3,2:T(8,128)(2,1)S(1)} copy(bf16[512,16,1,160]{0,3,1,2:T(8,128)(2,1)} %bitcast.42) | data formatting | bytes 5242880
  69.7 0.2 pad.1.clone
  70.0 0.0 copy-start.4
  70.0 1.5 %copy.18 = bf16[512,16,1,8,21]{0,3,4,1,2:T(8,128)(2,1)S(1)} copy(bf16[512,16,1,8,21]{0,1,4,3,2:T(8,128)(2,1)S(1)} %bitcast.39) | data formatting | bytes 5505024 | tf_op jit(solution)/shard_map/conv_general_dilated | solution.py:10
  71.5 0.1 slice.29
  71.6 6.8 %fusion.9 = f32[16,8,21,128]{3,1,2,0:T(8,128)S(1)} fusion(bf16[128,3,3,512]{0,3,2,1:T(8,128)(2,1)S(1)} %bitcast.45, bf16[512,16,1,7,2]{0,3,4,1,2:T(8,128)(2,1)S(1)} %slice.29, bf16[512,16,1,8,21]{0,3,4,1,2:T(8,128)(2,1)S(1)} %copy.18, pred[8,21]{0,1:T(8,128)(4,1)S(1)} %copy-done.4), kind=kOutput, calls=%fused_computation.9 | convolution fusion | flops 3048161280 | bytes 5537960 | tf_op jit(solution)/shard_map/conv_general_dilated | solution.py:10
  78.4 0.3 copy.20
  78.6 0.1 slice_bitcast_fusion
  78.7 0.0 copy-start.2
  78.7 0.4 copy.21
  79.2 0.2 copy-done.2
  79.4 1.0 fusion.17
  80.3 3.7 %all-to-all-start = ((bf16[1,128,8,320]{1,3,0,2:T(8,128)(2,1)}), bf16[1,128,8,320]{1,3,0,2:T(8,128)(2,1)S(1)}, u32[]{:S(2)}, u32[]{:S(2)}) async-start(bf16[1,128,8,320]{1,3,0,2:T(8,128)(2,1)} %fusion.17), calls=%async_computation | async-start | bytes 1310720 | tf_op jit(solution)/shard_map/all_to_all | solution.py:51
  84.0 0.0 copy-start.3
  84.0 11.1 %all-to-all-done = bf16[1,128,8,320]{1,3,0,2:T(8,128)(2,1)S(1)} async-done(((bf16[1,128,8,320]{1,3,0,2:T(8,128)(2,1)}), bf16[1,128,8,320]{1,3,0,2:T(8,128)(2,1)S(1)}, u32[]{:S(2)}, u32[]{:S(2)}) %all-to-all-start) | async-done | bytes 655392 | tf_op jit(solution)/shard_map/all_to_all | solution.py:51
  95.1 0.1 pad_convert_fusion
  95.2 0.3 fusion.18
  95.6 13.5 %all_to_all.33 = bf16[8,128,1,320]{1,3,2,0:T(8,128)(2,1)S(1)} all-to-all(bf16[8,128,1,320]{1,3,2,0:T(8,128)(2,1)S(1)} %fusion.18), channel_id=1, replica_groups=mesh['frame'=8,'chan'=4] {'frame'}, dimensions={0} | all-to-all | bytes 1310720 | tf_op jit(solution)/shard_map/all_to_all | solution.py:54
  109.1 1.1 copy.24
  (7 shorter events, 0.0 us)
Async XLA Ops:
  6.5 2.3 %copy-start = (bf16[128,4608]{1,0:T(8,128)(2,1)S(1)}, bf16[128,4608]{1,0:T(8,128)(2,1)}, u32[]{:S(2)}) copy-start(bf16[128,4608]{1,0:T(8,128)(2,1)} %param.6) | copy-start | bytes 3538948
  6.5 60.0 %all-gather.2.cloned.1.call-start = ((), (), s32[]{:S(2)}) async-start(), calls=%async_computation.2 | async-start | bytes 3276800 | tf_op jit(solution)/shard_map/all_gather | solution.py:41
  70.0 1.6 %copy-start.4 = (pred[8,21]{0,1:T(8,128)(4,1)S(1)}, pred[8,21]{0,1:T(8,128)(4,1)}, u32[]{:S(2)}) copy-start(pred[8,21]{0,1:T(8,128)(4,1)} %constant.9) | copy-start | bytes 508
  78.7 0.7 copy-start.2
  79.4 4.6 %copy-start.1 = (f32[3,128]{1,0:T(4,128)S(1)}, f32[3,128]{1,0:T(4,128)}, u32[]{:S(2)}) copy-start(f32[3,128]{1,0:T(4,128)} %param.8) | copy-start | bytes 4612
  80.3 14.8 %all-to-all-start = ((bf16[1,128,8,320]{1,3,0,2:T(8,128)(2,1)}), bf16[1,128,8,320]{1,3,0,2:T(8,128)(2,1)S(1)}, u32[]{:S(2)}, u32[]{:S(2)}) async-start(bf16[1,128,8,320]{1,3,0,2:T(8,128)(2,1)} %fusion.17), calls=%async_computation | async-start | bytes 1310720 | tf_op jit(solution)/shard_map/all_to_all | solution.py:51
  84.0 11.2 %copy-start.3 = (f32[128]{0:T(128)S(1)}, f32[128]{0:T(128)}, u32[]{:S(2)}) copy-start(f32[128]{0:T(128)} %param.9) | copy-start | bytes 1540
Sparse Core Ops, SparseCore 0:
  8.9 57.5 all-gather.1
where the time goes:
time: 117 us
  waiting for transfers between devices  68.1 us (58%)
  blocking collectives  13.5 us (12%)
  between operations  13.5 us (12%)
  local copies, waits for them, and re-layouts  10.1 us (9%)
  matrix products  6.76 us (6%)
  starting transfers between devices  3.67 us (3%)
  other arithmetic  1.36 us (1%)
    all_gather x1, waiting for transfers between devices, shards(): piece = lax.all_gather(latent, 'chan', axis=1, tiled=True)  57 us
    all_to_all x1, blocking collectives, shards(): lax.all_to_all(filtered, 'frame', split_axis=0, concat_axis=2, tiled=True)  13.5 us
    all_to_all x1, waiting for transfers between devices, shards(): lax.all_to_all(banded, 'frame', split_axis=2, concat_axis=0, tiled=True)  11.1 us
    conv_general_dilated x1, matrix products, convolve(): lax.conv_general_dilated(image, filters, (1, 1), padding, dimension_numbe...  6.76 us
    unnamed x13, local copies, waits for them, and re-layouts  6.42 us
    all_to_all x1, starting transfers between devices, shards(): lax.all_to_all(banded, 'frame', split_axis=2, concat_axis=0, tiled=True)  3.66 us
    conv_general_dilated x5, local copies, waits for them, and re-layouts, convolve(): lax.conv_general_dilated(image, filters, (1, 1), padding, dimension_numbe...  2.37 us
  transfers between devices with their start and end apart: 2, of which 2 were waited for; matrix products, arithmetic and copies ran while one was open for 1% of the time, Pallas kernels for 0%

commit v1 on v0

--- a/solution.py
+++ b/solution.py
@@ -48,7 +48,10 @@
     spatial = (summed + spatial_b[None, :, None]).astype(jnp.bfloat16)
     band_count = lax.axis_size("frame")
     banded = spatial.reshape(frames, local_chan, band_count, pixels // band_count)
-    band = lax.all_to_all(banded, "frame", split_axis=2, concat_axis=0, tiled=True)
+    band = jnp.concatenate(
+        lax.all_to_all(jnp.stack(jnp.split(banded, lax.axis_size("frame"), axis=2)), "frame", 0, 0),
+        axis=0,
+    )
     zeros = jnp.zeros((2,) + band.shape[1:], jnp.bfloat16)
     filtered = three_taps(zeros, band, temporal_w, temporal_b)
     result = lax.all_to_all(filtered, "frame", split_axis=0, concat_axis=2, tiled=True)

time: 117 us -> 122 us (1.043)
  local copies, waits for them, and re-layouts: 10.1 us -> 15.3 us
    unnamed x13 -> x20, local copies, waits for them, and re-layouts: 6.42 us -> 10.9 us
where the time goes in v1:
time: 122 us; the launch traced here: 121 us
  waiting for transfers between devices  68.1 us (56%)
  local copies, waits for them, and re-layouts  15.3 us (13%)
  blocking collectives  13.5 us (11%)
  between operations  13.5 us (11%)
  matrix products  6.76 us (6%)
  starting transfers between devices  3.67 us (3%)
    all_gather x1, waiting for transfers between devices, shards(): piece = lax.all_gather(latent, 'chan', axis=1, tiled=True)  57 us
    all_to_all x1, blocking collectives, shards(): lax.all_to_all(filtered, 'frame', split_axis=0, concat_axis=2, tiled=True)  13.5 us
    all_to_all x1, waiting for transfers between devices, shards(): lax.all_to_all(jnp.stack(jnp.split(banded, lax.axis_size('frame'), axis=2...  11.1 us
    unnamed x20, local copies, waits for them, and re-layouts  10.9 us
    conv_general_dilated x1, matrix products, convolve(): lax.conv_general_dilated(image, filters, (1, 1), padding, dimension_numbe...  6.76 us
    all_to_all x1, starting transfers between devices, shards(): lax.all_to_all(jnp.stack(jnp.split(banded, lax.axis_size('frame'), axis=2...  3.66 us
  transfers between devices with their start and end apart: 2, of which 2 were waited for; matrix products, arithmetic and copies ran while one was open for 1% of the time, Pallas kernels for 0%

profile of v1, /device:TPU:0, one launch (start us, length us, event | category | flops | bytes accessed | tf_op | source)
XLA Modules:
  0.0 121.3 jit_solution(1209879732025617245)
XLA Ops:
  6.5 2.3 %copy.22 = bf16[1,128,2560]{1,2,0:T(8,128)(2,1)} copy(bf16[1,128,2560]{2,1,0:T(8,128)(2,1)} %param.5) | data formatting | bytes 1310720 | tf_op args[0]
  8.8 0.7 copy.26
  9.6 57.0 %all-gather.2.cloned.1.call-done = bf16[1,512,2560]{1,2,0:T(8,128)(2,1)} async-done(((bf16[1,128,2560]{1,2,0:T(8,128)(2,1)}), bf16[1,512,2560]{1,2,0:T(8,128)(2,1)}) %all-gather.2.cloned.1.call-update) | async-done | bytes 2621456 | tf_op jit(solution)/shard_map/all_gather | solution.py:41
  66.5 3.2 %copy.31 = bf16[512,16,1,160]{0,1,3,2:T(8,128)(2,1)S(1)} copy(bf16[512,16,1,160]{0,3,1,2:T(8,128)(2,1)} %bitcast.66) | data formatting | bytes 5242880
  69.7 0.2 pad.1.clone
  70.0 1.5 %copy.25 = bf16[512,16,1,8,21]{0,3,4,1,2:T(8,128)(2,1)S(1)} copy(bf16[512,16,1,8,21]{0,1,4,3,2:T(8,128)(2,1)S(1)} %bitcast.63) | data formatting | bytes 5505024 | tf_op jit(solution)/shard_map/conv_general_dilated | solution.py:10
  71.6 6.8 %fusion.9 = f32[16,8,21,128]{3,1,2,0:T(8,128)S(1)} fusion(bf16[128,3,3,512]{0,3,2,1:T(8,128)(2,1)S(1)} %bitcast.69, bf16[512,16,1,7,2]{0,3,4,1,2:T(8,128)(2,1)S(1)} %slice.29, bf16[512,16,1,8,21]{0,3,4,1,2:T(8,128)(2,1)S(1)} %copy.25, pred[8,21]{0,1:T(8,128)(4,1)S(1)} %copy-done.4), kind=kOutput, calls=%fused_computation.9 | convolution fusion | flops 3048161280 | bytes 5537960 | tf_op jit(solution)/shard_map/conv_general_dilated | solution.py:10
  78.4 0.3 copy.27
  78.7 0.4 copy.28
  79.2 0.2 copy-done.2
  79.4 0.1 fusion.16
  79.5 0.6 fusion.25
  80.2 0.6 fusion.24
  80.8 0.6 fusion.23
  81.4 0.6 fusion.22
  82.1 0.6 fusion.21
  82.7 0.6 fusion.20
  83.4 0.6 fusion.19
  84.0 0.6 fusion.18
  84.7 3.7 %all-to-all-start = ((bf16[8,1,128,1,320]{2,4,3,1,0:T(8,128)(2,1)}), bf16[8,1,128,1,320]{2,4,3,1,0:T(8,128)(2,1)S(1)}, u32[]{:S(2)}, u32[]{:S(2)}) async-start(bf16[8,1,128,1,320]{2,4,3,1,0:T(8,128)(2,1)} %fusion.18), calls=%async_computation | async-start | bytes 1310720 | tf_op jit(solution)/shard_map/all_to_all | solution.py:52
  88.3 11.1 %all-to-all-done = bf16[8,1,128,1,320]{2,4,3,1,0:T(8,128)(2,1)S(1)} async-done(((bf16[8,1,128,1,320]{2,4,3,1,0:T(8,128)(2,1)}), bf16[8,1,128,1,320]{2,4,3,1,0:T(8,128)(2,1)S(1)}, u32[]{:S(2)}, u32[]{:S(2)}) %all-to-all-start) | async-done | bytes 655392 | tf_op jit(solution)/shard_map/all_to_all | solution.py:52
  99.6 0.3 fusion.17
  99.9 13.5 %all_to_all.20 = bf16[8,128,1,320]{1,3,2,0:T(8,128)(2,1)S(1)} all-to-all(bf16[8,128,1,320]{1,3,2,0:T(8,128)(2,1)S(1)} %fusion.17), channel_id=1, replica_groups=mesh['frame'=8,'chan'=4] {'frame'}, dimensions={0} | all-to-all | bytes 1310720 | tf_op jit(solution)/shard_map/all_to_all | solution.py:57
  113.4 1.1 copy.30
  (15 shorter events, 0.3 us)
Async XLA Ops:
  6.5 2.3 %copy-start = (bf16[128,4608]{1,0:T(8,128)(2,1)S(1)}, bf16[128,4608]{1,0:T(8,128)(2,1)}, u32[]{:S(2)}) copy-start(bf16[128,4608]{1,0:T(8,128)(2,1)} %param.6) | copy-start | bytes 3538948
  6.5 60.0 %all-gather.2.cloned.1.call-start = ((), (), s32[]{:S(2)}) async-start(), calls=%async_computation.2 | async-start | bytes 3276800 | tf_op jit(solution)/shard_map/all_gather | solution.py:41
  70.0 1.6 %copy-start.4 = (pred[8,21]{0,1:T(8,128)(4,1)S(1)}, pred[8,21]{0,1:T(8,128)(4,1)}, u32[]{:S(2)}) copy-start(pred[8,21]{0,1:T(8,128)(4,1)} %constant.9) | copy-start | bytes 508
  78.7 0.7 copy-start.2
  79.5 8.8 %copy-start.1 = (f32[3,128]{1,0:T(4,128)S(1)}, f32[3,128]{1,0:T(4,128)}, u32[]{:S(2)}) copy-start(f32[3,128]{1,0:T(4,128)} %param.8) | copy-start | bytes 4612
  84.7 14.8 %all-to-all-start = ((bf16[8,1,128,1,320]{2,4,3,1,0:T(8,128)(2,1)}), bf16[8,1,128,1,320]{2,4,3,1,0:T(8,128)(2,1)S(1)}, u32[]{:S(2)}, u32[]{:S(2)}) async-start(bf16[8,1,128,1,320]{2,4,3,1,0:T(8,128)(2,1)} %fusion.18), calls=%async_computation | async-start | bytes 1310720 | tf_op jit(solution)/shard_map/all_to_all | solution.py:52
  88.3 11.2 %copy-start.3 = (f32[128]{0:T(128)S(1)}, f32[128]{0:T(128)}, u32[]{:S(2)}) copy-start(f32[128]{0:T(128)} %param.9) | copy-start | bytes 1540
Sparse Core Ops, SparseCore 0:
  8.9 57.5 all-gather.1
